TPU v7x, 512 devices: a whole 4x4x16 slice. The times are simulated.
512 devices in a mesh: req: 128 (over y, z, core), tp: 4 (over x).
Axes of the slice: x: 4, y: 4, z: 16, core: 2. Of those that a mesh axis runs over, the one named last changes fastest.
Arguments:
- queries: bfloat16 [32768, 2048], P('req', 'tp'), may hold values from -160 to 160
- key_rows: bfloat16 [32768, 2048], P('req', 'tp'), may hold values from -6 to 6
- value_rows: bfloat16 [32768, 2048], P('req', 'tp'), may hold values from -6 to 6
- lengths: int32 [128, 4], P('req'), may hold values from 1 to 128, 256 in all within a row
- adapter_ids: int32 [128, 4], P('req'), may hold values from 0 to 127, as said below
- adapter_home: int32 [128], replicated, may hold values from 0 to 127, each once
- adapter_down: bfloat16 [128, 2048, 16], P('req', 'tp'), may hold values from -0.125 to 0.125
- adapter_up: bfloat16 [128, 16, 2048], P('req'), may hold values from -4 to 4
- output_weight: bfloat16 [2048, 2048], P('tp'), may hold values from -0.125 to 0.125
Outputs:
- block_output: bfloat16 [32768, 2048], P('req', 'tp')
Inputs may be any that keep to these rules, and one draw needn't show every extreme that they name: `adapter_ids`: all prompts together name exactly 16 distinct adapters.
All inputs are finite; a program needn't handle non-finite values.
Results may differ from a plain program's by a relative error of at most 0.0055.
Values may be sent and summed in bfloat16 or wider, within the bound.
A program may use at most 64 MiB of HBM per device.

v0:
```python
import math

import jax
import jax.numpy as jnp
from jax import lax
from jax.sharding import PartitionSpec as P

HD = 128


def segment_rows(length_row, row_total):
    boundary = jnp.cumsum(length_row)
    position = jnp.arange(row_total, dtype=jnp.int32)
    return jnp.sum((position[:, None] >= boundary[None, :]).astype(jnp.int32), axis=1)


def attend(queries, key_rows, value_rows, segment):
    row_total = queries.shape[0]
    head_count = queries.shape[1] // HD
    shaped_q = queries.reshape(row_total, head_count, HD)
    shaped_k = key_rows.reshape(row_total, head_count, HD)
    shaped_v = value_rows.reshape(row_total, head_count, HD)
    scores = jnp.einsum("qhd,khd->hqk", shaped_q, shaped_k, preferred_element_type=jnp.float32) * (
        1.0 / math.sqrt(HD)
    )
    position = jnp.arange(row_total, dtype=jnp.int32)
    allowed = (segment[:, None] == segment[None, :]) & (position[None, :] <= position[:, None])
    masked = jnp.where(allowed[None], scores, -1e30)
    highest = jnp.max(masked, axis=2, keepdims=True)
    exponent = jnp.where(allowed[None], jnp.exp(masked - highest), 0.0)
    weights = (exponent / jnp.sum(exponent, axis=2, keepdims=True)).astype(jnp.bfloat16)
    mixed = jnp.einsum("hqk,khd->qhd", weights, shaped_v, preferred_element_type=jnp.float32)
    return mixed.reshape(row_total, head_count * HD).astype(jnp.bfloat16)


def lowrank_delta(rank_rows, onehot, factor_up):
    row_total, prompts = onehot.shape
    rank_size = rank_rows.shape[1]
    spread = (onehot[:, :, None] * rank_rows[:, None, :]).reshape(row_total, prompts * rank_size)
    upper = factor_up.astype(jnp.float32).reshape(prompts * rank_size, factor_up.shape[2])
    return jnp.dot(spread, upper, precision=lax.Precision.HIGHEST)


def body(
    queries,
    key_rows,
    value_rows,
    lengths,
    adapter_ids,
    adapter_home,
    adapter_down,
    adapter_up,
    output_weight,
):
    row_total = queries.shape[0]
    prompts = lengths.shape[1]
    segment = segment_rows(lengths[0], row_total)
    prompt_ids = adapter_ids[0]
    downs_all, uppers_all = (
        lax.all_gather(adapter_down, "req", axis=0, tiled=True),
        lax.all_gather(adapter_up, "req", axis=0, tiled=True),
    )
    slot_rows = adapter_home[prompt_ids]
    downs = downs_all[slot_rows]
    uppers = uppers_all[slot_rows]
    attended = attend(queries, key_rows, value_rows, segment)
    onehot = (segment[:, None] == jnp.arange(prompts, dtype=jnp.int32)[None, :]).astype(jnp.float32)
    per_prompt = jnp.einsum("ta,sar->str", attended, downs, preferred_element_type=jnp.float32)
    low_local = jnp.einsum("ts,str->tr", onehot, per_prompt, precision=lax.Precision.HIGHEST)
    base_rows = jnp.dot(attended, output_weight, preferred_element_type=jnp.float32)
    partial_rows = base_rows + lowrank_delta(low_local, onehot, uppers)
    summed = lax.psum_scatter(partial_rows, "tp", scatter_dimension=1, tiled=True)
    return summed.astype(jnp.bfloat16)


def solution(mesh):
    return jax.shard_map(
        body,
        mesh=mesh,
        in_specs=(
            P("req", "tp"),
            P("req", "tp"),
            P("req", "tp"),
            P("req", None),
            P("req", None),
            P(),
            P("req", "tp", None),
            P("req", None, None),
            P("tp", None),
        ),
        out_specs=P("req", "tp"),
        check_vma=False,
    )
```

profile of v0, /device:TPU:1, one launch (start us, length us, event | category | flops | bytes accessed | tf_op | source)
XLA Modules:
  0.0 350.7 jit_solution(13716006195187594143)
XLA Ops:
  6.5 0.0 copy-start
  6.5 0.0 all-gather.3.cloned.1.call-start
  6.5 0.7 all-gather.3.cloned.1.call-update
  7.3 0.0 all-gather.5.cloned.1.call-start
  7.3 0.7 all-gather.5.cloned.1.call-update
  8.0 0.0 copy-start.1
  8.0 0.0 reduce-scatter.2.cloned.1.call-start
  8.1 1.8 copy.35
  9.9 0.7 fusion.20
  10.6 1.3 gather_fusion
  11.8 0.8 reduce-window.8
  12.7 0.1 convert_reduce_fusion
  12.8 0.1 fusion.11
  12.9 1.6 fusion.26
  14.5 0.0 copy-done.1
  14.5 1.3 fusion.4
  15.8 1.4 convolution_convert_fusion
  17.2 139.8 %all-gather.3.cloned.1.call-done = bf16[128,512,16]{1,2,0:T(8,128)(2,1)} async-done(((bf16[1,512,16]{1,2,0:T(8,128)(2,1)}), bf16[128,512,16]{1,2,0:T(8,128)(2,1)}) %all-gather.3.cloned.1.call-update) | async-done | bytes 2097168 | tf_op jit(solution)/shard_map/all_gather | solution.py:60
  157.0 2.1 gather_fusion.1
  159.1 0.2 fusion.6
  159.3 144.2 %all-gather.5.cloned.1.call-done = bf16[128,16,2048]{2,1,0:T(8,128)(2,1)} async-done(((bf16[1,16,2048]{2,1,0:T(8,128)(2,1)}), bf16[128,16,2048]{2,1,0:T(8,128)(2,1)}) %all-gather.5.cloned.1.call-update) | async-done | bytes 8388624 | tf_op jit(solution)/shard_map/all_gather | solution.py:61
  303.5 3.9 %gather_fusion.2 = bf16[4,16,2048]{2,1,0:T(8,128)(2,1)S(1)} fusion(bf16[128,16,2048]{2,1,0:T(8,128)(2,1)} %all-gather.5.cloned.1.call-done, s32[1024]{0:T(1024)S(1)} %pad_clamp_fusion), kind=kCustom, calls=%fused_computation.2 | custom fusion | bytes 524304 | tf_op jit(solution)/shard_map/gather | solution.py:65
  307.5 1.0 convolution_bitcast_fusion
  308.5 0.0 copy-done
  308.5 2.1 convolution_add_fusion
  310.6 0.0 reduce-scatter.2.cloned.1.call-update
  310.6 31.8 %reduce-scatter.2.cloned.1.call-done = f32[256,512]{1,0:T(8,128)} async-done(((f32[256,2048]{1,0:T(8,128)}), f32[256,512]{1,0:T(8,128)}) %reduce-scatter.2.cloned.1.call-update) | async-done | bytes 524304 | tf_op jit(solution)/shard_map/reduce_scatter | solution.py:72
  342.4 1.8 convert_element_type.32
  (4 shorter events, 0.0 us)
Async XLA Ops:
  6.5 302.0 %copy-start = (bf16[512,2048]{1,0:T(8,128)(2,1)S(1)}, bf16[512,2048]{1,0:T(8,128)(2,1)}, u32[]{:S(2)}) copy-start(bf16[512,2048]{1,0:T(8,128)(2,1)} %param.17) | copy-start | bytes 6291460
  6.5 150.4 %all-gather.3.cloned.1.call-start = ((), (), s32[]{:S(2)}) async-start(), calls=%async_computation.1 | async-start | bytes 2113536 | tf_op jit(solution)/shard_map/all_gather | solution.py:60
  7.3 296.3 %all-gather.5.cloned.1.call-start = ((), (), s32[]{:S(2)}) async-start(), calls=%async_computation.2 | async-start | bytes 8454144 | tf_op jit(solution)/shard_map/all_gather | solution.py:61
  8.0 6.5 %copy-start.1 = (bf16[256,512]{1,0:T(8,128)(2,1)S(1)}, bf16[256,512]{1,0:T(8,128)(2,1)}, u32[]{:S(2)}) copy-start(bf16[256,512]{1,0:T(8,128)(2,1)} %param.10) | copy-start | bytes 786436
  8.0 334.4 %reduce-scatter.2.cloned.1.call-start = ((), (), s32[]{:S(2)}) async-start(), calls=%async_computation.3 | async-start | bytes 2621440 | tf_op jit(solution)/shard_map/reduce_scatter | solution.py:72
Sparse Core Ops, SparseCore 0:
  10.5 146.4 all-gather.2
  160.1 143.3 all-gather.4
  310.8 31.6 reduce-scatter.1
where the time goes:
time: 351 us
  waiting for transfers between devices  317 us (90%)
  between operations  13.2 us (4%)
  local copies, waits for them, and re-layouts  9.21 us (3%)
  matrix products  7.58 us (2%)
    all_gather x1, waiting for transfers between devices, body(): lax.all_gather(adapter_up, 'req', axis=0, tiled=True)  144 us
    all_gather x1, waiting for transfers between devices, body(): lax.all_gather(adapter_down, 'req', axis=0, tiled=True)  140 us
    reduce_scatter x1, waiting for transfers between devices, body(): lax.psum_scatter(partial_rows, 'tp', scatter_dimension=1, tiled=True)  31.8 us
  transfers between devices with their start and end apart: 3, of which 3 were waited for; matrix products, arithmetic and copies ran while one was open for 3% of the time, Pallas kernels for 0%

commit v1 on v0

v1 whole, which is shorter than its diff:
```python
import math

import jax
import jax.numpy as jnp
from jax import lax
from jax.experimental import pallas as pl
from jax.experimental.pallas import tpu as pltpu
from jax.sharding import PartitionSpec as P

HD = 128
NY, NZ = 4, 16
LINE = NY * NZ
MESH = pl.DeviceIdType.MESH
F32 = jnp.float32
BF16 = jnp.bfloat16


def stage_offsets(stage):
    if stage == 0:
        return (0,)
    far, near = 2 * stage, 2 * stage - 1
    if far == NZ // 2:
        return (far, NZ - near, near)
    return (NZ - far, far, NZ - near, near)


def kernel(
    len_s,
    ids_s,
    home_s,
    q_h,
    k_h,
    v_h,
    dn_h,
    up_h,
    w_h,
    out_ref,
    qv,
    kv,
    vv,
    wv,
    gd,
    gu,
    att,
    part,
    got,
    fwd_part,
    acc,
    slot_send,
    slot_got,
    slot_s,
    sel_send,
    sel_got,
    low_own,
    low_got,
    load_sem,
    g_send,
    z_recv,
    y_recv,
    o_recv,
    x_send,
    x_recv,
    slot_sem,
    sel_sem,
    low_send,
    low_recv,
):
    req = lax.axis_index("req")
    x = lax.axis_index("tp")
    core = lax.rem(req, 2)
    z = lax.rem(lax.div(req, 2), NZ)
    y = lax.div(req, 2 * NZ)
    rows, width = qv.shape
    half = rows // 2
    prompts = ids_s.shape[1]

    def place(y_at, z_at, core_at):
        return (y_at * NZ + z_at) * 2 + core_at

    def shifted(at, by, size):
        return lax.rem(at + (by + size) % size, size)

    def z_peer(by):
        return (place(y, shifted(z, by, NZ), core), x)

    def y_peer(by):
        return (place(shifted(y, by, NY), z, core), x)

    def x_peer(by):
        return (req, shifted(x, by, 4))

    partner = (place(y, z, 1 - core), x)

    def line(y_by, offset):
        return shifted(y, y_by, NY) * NZ + shifted(z, offset, NZ)

    def remote(src, dst, send, recv, device):
        return pltpu.make_async_remote_copy(
            src_ref=src, dst_ref=dst, send_sem=send, recv_sem=recv, device_id=device, device_id_type=MESH
        )

    banks = (gd, gu)
    own_line = line(0, 0)

    barrier = pltpu.get_barrier_semaphore()
    peers = [z_peer(b) for b in (1, -1, 2, -2)] + [y_peer(1), y_peer(-1), partner] + [x_peer(b) for b in (1, 2, 3)]
    for peer in peers:
        pl.semaphore_signal(barrier, inc=1, device_id=peer, device_id_type=MESH)
    columns = pl.ds(pl.multiple_of(x * width, width), width)
    loads = [
        pltpu.make_async_copy(dn_h.at[0], gd.at[own_line], load_sem.at[0]),
        pltpu.make_async_copy(up_h.at[0, :, columns], gu.at[own_line], load_sem.at[1]),
        pltpu.make_async_copy(q_h, qv, load_sem.at[2]),
        pltpu.make_async_copy(k_h, kv, load_sem.at[3]),
        pltpu.make_async_copy(v_h, vv, load_sem.at[4]),
        pltpu.make_async_copy(w_h, wv, load_sem.at[5]),
    ]
    for load in loads:
        load.start()

    lane = lax.broadcasted_iota(jnp.int32, (8, 128), 1)
    slots = jnp.zeros((8, 128), jnp.int32)
    own_slots = []
    for s in range(prompts):
        home = home_s[ids_s[0, s]]
        own_slots.append(home)
        slots = jnp.where(lane == s, home, slots)
    slot_send[...] = slots

    loads[0].wait()
    loads[1].wait()
    pl.semaphore_wait(barrier, len(peers))

    def z_send(p, offset, by):
        j = line(0, offset)
        remote(
            banks[p].at[j], banks[p].at[j], g_send.at[p], z_recv.at[p, (offset - by) % NZ], z_peer(by)
        ).start()

    def y_send(p, offset):
        j = line(0, offset)
        for way, by in ((0, 1), (1, -1)):
            remote(banks[p].at[j], banks[p].at[j], g_send.at[p], y_recv.at[p, way, offset], y_peer(by)).start()

    def own_sends(p):
        for by in (2, -2, 1, -1):
            z_send(p, 0, by)
        y_send(p, 0)

    def z_stage(p, stage):
        for offset in stage_offsets(stage):
            j = line(0, offset)
            remote(banks[p].at[j], banks[p].at[j], g_send.at[p], z_recv.at[p, offset], z_peer(1)).wait_recv()
            distance = min(offset, NZ - offset)
            if distance == 2 * stage and distance < NZ // 2:
                if offset > NZ // 2:
                    z_send(p, offset, 2)
                    z_send(p, offset, 1)
                else:
                    if distance + 2 < NZ // 2:
                        z_send(p, offset, -2)
                    z_send(p, offset, -1)
            y_send(p, offset)

    def y_stage(p, stage):
        for offset in stage_offsets(stage):
            for way, by in ((0, 1), (1, -1)):
                j = line(-by, offset)
                bank = banks[p].at[j]
                remote(bank, bank, g_send.at[p], y_recv.at[p, way, offset], y_peer(by)).wait_recv()
                if offset % 2 == way:
                    remote(bank, bank, g_send.at[p], o_recv.at[p, offset], y_peer(by)).start()

    def o_stage(p, stage):
        for offset in stage_offsets(stage):
            bank = banks[p].at[line(2, offset)]
            remote(bank, bank, g_send.at[p], o_recv.at[p, offset], y_peer(1)).wait_recv()

    starts = []
    edge = jnp.int32(0)
    for s in range(prompts - 1):
        edge = edge + len_s[0, s]
        starts.append(edge)

    def allowed_of(first, count, keys):
        row = lax.broadcasted_iota(jnp.int32, (count, keys), 0) + first
        key = lax.broadcasted_iota(jnp.int32, (count, keys), 1)
        begin = jnp.zeros((count, keys), jnp.int32)
        for start in starts:
            begin = jnp.where(row >= start, start, begin)
        return (key <= row) & (key >= begin)

    def attend(head, first, keys, allowed):
        cols = slice(head * HD, (head + 1) * HD)
        scores = lax.dot_general(
            qv[first : first + half, cols],
            kv[:keys, cols],
            (((1,), (1,)), ((), ())),
            preferred_element_type=F32,
        ) * (1.0 / math.sqrt(HD))
        masked = jnp.where(allowed, scores, -1e30)
        highest = jnp.max(masked, axis=1, keepdims=True)
        exponent = jnp.exp(masked - highest)
        weights = (exponent * (1.0 / jnp.sum(exponent, axis=1, keepdims=True))).astype(BF16)
        mixed = jnp.dot(weights, vv[:keys, cols], preferred_element_type=F32)
        att[first : first + half, cols] = mixed.astype(BF16)

    def project(first, count, by):
        cols = pl.ds(pl.multiple_of(shifted(x, by, 4) * width, width), width)
        return jnp.dot(att[first : first + count, :], wv[:, cols], preferred_element_type=F32)

    top, low = slice(0, half), slice(half, rows)

    def x_copy(slot, src, dst, by):
        return remote(src, dst, x_send.at[slot], x_recv.at[slot], x_peer(by))

    def x_copies():
        return (
            x_copy(0, part.at[0, top], fwd_part.at[top], 1),
            x_copy(1, part.at[0, low], fwd_part.at[low], -1),
            x_copy(2, part.at[1, top], got.at[0, top], 1),
            x_copy(3, part.at[1, low], got.at[0, low], 1),
            x_copy(4, part.at[2, top], got.at[1, top], -1),
            x_copy(5, part.at[2, low], got.at[1, low], -1),
        )

    xc = x_copies()

    own_sends(0)
    own_sends(1)
    slot_copy = remote(slot_send, slot_got, slot_sem.at[0], slot_sem.at[1], partner)
    slot_copy.start()

    for load in loads[2:5]:
        load.wait()
    allowed_top = allowed_of(0, half, half)
    for head in range(width // HD):
        attend(head, 0, half, allowed_top)
    loads[5].wait()
    part[0, top] = project(0, half, 2).astype(BF16)
    xc[0].start()
    allowed_low = allowed_of(half, half, rows)
    for head in range(width // HD):
        attend(head, half, rows, allowed_low)
    part[0, low] = project(half, half, 2).astype(BF16)
    xc[1].start()

    z_stage(0, 1)
    part[1, low] = project(half, half, 1).astype(BF16)
    xc[3].start()
    part[2, top] = project(0, half, -1).astype(BF16)
    xc[4].start()
    y_stage(0, 0)
    z_stage(1, 1)
    y_stage(1, 0)
    z_stage(0, 2)
    y_stage(0, 1)
    xc[0].wait_recv()
    part[1, top] = (project(0, half, 1) + fwd_part[top].astype(F32)).astype(BF16)
    xc[2].start()
    xc[1].wait_recv()
    part[2, low] = (project(half, half, -1) + fwd_part[low].astype(F32)).astype(BF16)
    xc[5].start()
    z_stage(1, 2)
    y_stage(1, 1)
    z_stage(0, 3)
    y_stage(0, 2)
    acc[...] = project(0, rows, 0)
    z_stage(1, 3)
    y_stage(1, 2)
    z_stage(0, 4)
    y_stage(0, 3)
    z_stage(1, 4)
    slot_copy.wait()
    slot_local = pltpu.make_async_copy(slot_got, slot_s, load_sem.at[6])
    slot_local.start()
    for c in (2, 3, 4, 5):
        xc[c].wait_recv()
    acc[...] += got[0].astype(F32) + got[1].astype(F32)
    slot_local.wait()
    y_stage(0, 4)
    for stage in range(5):
        o_stage(0, stage)

    def pick(p, home):
        return jnp.where(lax.rem(home, 2) == core, banks[p][lax.div(home, 2)], 0).astype(BF16)

    def select(p):
        for s in range(prompts):
            sel_send[p, s] = pick(p, slot_s[0, s])
        copy = remote(sel_send.at[p], sel_got.at[p], sel_sem.at[0, p], sel_sem.at[1, p], partner)
        copy.start()
        return copy

    def chosen(p):
        return jnp.concatenate([pick(p, own_slots[s]) + sel_got[p, s] for s in range(prompts)], axis=0)

    sel0 = select(0)
    y_stage(1, 3)
    sel0.wait()
    rank = gd.shape[1]
    spread = lax.dot_general(chosen(0), att[...], (((1,), (1,)), ((), ())), preferred_element_type=F32)
    token = lax.broadcasted_iota(jnp.int32, (rank, rows), 1)
    bounds = [0] + starts + [rows]

    def in_prompt(s):
        return (token >= bounds[s]) & (token < bounds[s + 1])

    mine = jnp.zeros((rank, rows), F32)
    for s in range(prompts):
        mine = mine + jnp.where(in_prompt(s), spread[s * rank : (s + 1) * rank, :], 0.0)
    low_own[...] = mine
    lows = [remote(low_own, low_got.at[i], low_send.at[i], low_recv.at[i], x_peer(i + 1)) for i in range(3)]
    for copy in lows:
        copy.start()
    y_stage(1, 4)
    for stage in range(5):
        o_stage(1, stage)
    sel1 = select(1)
    sel1.wait()
    factor_up = chosen(1).astype(F32)
    for copy in lows:
        copy.wait()
    total = low_own[...] + low_got[0] + low_got[1] + low_got[2]
    spread = jnp.concatenate([jnp.where(in_prompt(s), total, 0.0) for s in range(prompts)], axis=0)
    delta = jnp.dot(spread.T, factor_up, precision=lax.Precision.HIGHEST, preferred_element_type=F32)
    out_ref[...] = (acc[...] + delta).astype(BF16)

    for copy in xc:
        copy.wait_send()
    for p in range(2):
        sent = banks[p].at[pl.ds(0, LINE - 1)]
        remote(sent, sent, g_send.at[p], g_send.at[p], z_peer(1)).wait_send()


def body(queries, key_rows, value_rows, lengths, adapter_ids, adapter_home, adapter_down, adapter_up, output_weight):
    rows, width = queries.shape
    rank = adapter_up.shape[1]
    prompts = lengths.shape[1]
    dma = pltpu.SemaphoreType.DMA
    smem = pl.BlockSpec(memory_space=pltpu.SMEM)
    hbm = pl.BlockSpec(memory_space=pl.ANY)
    return pl.pallas_call(
        kernel,
        out_shape=jax.ShapeDtypeStruct((rows, width), BF16),
        in_specs=[smem] * 3 + [hbm] * 6,
        out_specs=pl.BlockSpec(memory_space=pltpu.VMEM),
        scratch_shapes=[
            pltpu.VMEM((rows, width), BF16),
            pltpu.VMEM((rows, width), BF16),
            pltpu.VMEM((rows, width), BF16),
            pltpu.VMEM(output_weight.shape, BF16),
            pltpu.VMEM((LINE, rank, width), BF16),
            pltpu.VMEM((LINE, rank, width), BF16),
            pltpu.VMEM((rows, width), BF16),
            pltpu.VMEM((3, rows, width), BF16),
            pltpu.VMEM((2, rows, width), BF16),
            pltpu.VMEM((rows, width), BF16),
            pltpu.VMEM((rows, width), F32),
            pltpu.VMEM((8, 128), jnp.int32),
            pltpu.VMEM((8, 128), jnp.int32),
            pltpu.SMEM((8, 128), jnp.int32),
            pltpu.VMEM((2, prompts, rank, width), BF16),
            pltpu.VMEM((2, prompts, rank, width), BF16),
            pltpu.VMEM((rank, rows), F32),
            pltpu.VMEM((3, rank, rows), F32),
            dma((7,)),
            dma((2,)),
            dma((2, NZ)),
            dma((2, 2, NZ)),
            dma((2, NZ)),
            dma((6,)),
            dma((6,)),
            dma((2,)),
            dma((2, 2)),
            dma((3,)),
            dma((3,)),
        ],
        compiler_params=pltpu.CompilerParams(
            collective_id=0, has_side_effects=True, vmem_limit_bytes=48 * 1024 * 1024
        ),
    )(
        lengths,
        adapter_ids,
        adapter_home,
        queries,
        key_rows,
        value_rows,
        jnp.swapaxes(adapter_down, 1, 2),
        adapter_up,
        output_weight,
    )


def solution(mesh):
    return jax.shard_map(
        body,
        mesh=mesh,
        in_specs=(
            P("req", "tp"),
            P("req", "tp"),
            P("req", "tp"),
            P("req", None),
            P("req", None),
            P(),
            P("req", "tp", None),
            P("req", None, None),
            P("tp", None),
        ),
        out_specs=P("req", "tp"),
        check_vma=False,
    )
```

time: 351 us -> 54 us (0.15)
  waiting for transfers between devices: 317 us -> 0 us
  Pallas kernels: 0 us -> 45 us
  between operations: 13.2 us -> 0.02 us
  matrix products: 7.58 us -> 0 us
    all_gather x2 -> x0, waiting for transfers between devices: 284 us -> none  [the longest x1 144 us: body(): lax.all_gather(adapter_up, 'req', axis=0, tiled=True)]
    pallas_call x0 -> x1, Pallas kernels: none -> 45 us  [body(): pl.pallas_call(kernel, out_shape=jax.ShapeDtypeStruct((rows, width), BF16...]
    reduce_scatter x1 -> x0, waiting for transfers between devices: 31.8 us -> none  [body(): lax.psum_scatter(partial_rows, 'tp', scatter_dimension=1, tiled=True)]
    unnamed x4 -> x19, local copies, waits for them, and re-layouts: 0.01 us -> 8.66 us
    gather x3 -> x0, local copies, waits for them, and re-layouts: 7.37 us -> none  [the longest x1 3.94 us: body(): uppers = uppers_all[slot_rows]]
    dot_general x5 -> x0, matrix products: 5.98 us -> none  [the longest x1 2.1 us: body(): jnp.dot(attended, output_weight, preferred_element_type=jnp.float32)]
  transfers between devices with their start and end apart: 3 -> 0, of which waited for: 3 -> 0; matrix products, arithmetic and copies ran while one was open for 3% -> 0% of each run, Pallas kernels for 0% -> 0%
where the time goes in v1:
time: 54 us; the launch traced here: 53.7 us
  Pallas kernels  45 us (83%)
  local copies, waits for them, and re-layouts  8.66 us (16%)
    pallas_call x1, Pallas kernels, body(): pl.pallas_call(kernel, out_shape=jax.ShapeDtypeStruct((rows, width), BF16...  45 us
    unnamed x19, local copies, waits for them, and re-layouts  8.66 us

profile of v1, /device:TPU:1, one launch (start us, length us, event | category | flops | bytes accessed | tf_op | source)
XLA Modules:
  0.0 53.7 jit_solution(3386230780832352077)
XLA Ops:
  0.0 0.0 copy-start
  0.0 1.6 %copy-done = bf16[512,2048]{1,0:T(8,128)(2,1)S(1)} copy-done((bf16[512,2048]{1,0:T(8,128)(2,1)S(1)}, bf16[512,2048]{1,0:T(8,128)(2,1)}, u32[]{:S(2)}) %copy-start) | copy-done | bytes 2097176
  1.6 0.0 copy-start.1
  1.6 0.9 %copy-done.1 = bf16[256,512]{1,0:T(8,128)(2,1)S(1)} copy-done((bf16[256,512]{1,0:T(8,128)(2,1)S(1)}, bf16[256,512]{1,0:T(8,128)(2,1)}, u32[]{:S(2)}) %copy-start.1) | copy-done | bytes 262168
  2.5 0.0 copy-start.2
  2.5 0.9 %copy-done.2 = bf16[256,512]{1,0:T(8,128)(2,1)S(1)} copy-done((bf16[256,512]{1,0:T(8,128)(2,1)S(1)}, bf16[256,512]{1,0:T(8,128)(2,1)}, u32[]{:S(2)}) %copy-start.2) | copy-done | bytes 262168
  3.5 0.0 copy-start.3
  3.5 0.9 %copy-done.3 = bf16[256,512]{1,0:T(8,128)(2,1)S(1)} copy-done((bf16[256,512]{1,0:T(8,128)(2,1)S(1)}, bf16[256,512]{1,0:T(8,128)(2,1)}, u32[]{:S(2)}) %copy-start.3) | copy-done | bytes 262168
  4.4 0.0 copy-start.4
  4.4 0.8 %copy-done.4 = bf16[1,16,2048]{2,1,0:T(8,128)(2,1)S(1)} copy-done((bf16[1,16,2048]{2,1,0:T(8,128)(2,1)S(1)}, bf16[1,16,2048]{2,1,0:T(8,128)(2,1)}, u32[]{:S(2)}) %copy-start.4) | copy-done | bytes 65560
  5.3 0.0 copy-start.5
  5.3 0.7 %copy-done.5 = bf16[1,512,16]{1,2,0:T(8,128)(2,1)S(1)} copy-done((bf16[1,512,16]{1,2,0:T(8,128)(2,1)S(1)}, bf16[1,512,16]{1,2,0:T(8,128)(2,1)}, u32[]{:S(2)}) %copy-start.5) | copy-done | bytes 16408
  6.0 0.0 copy-start.6
  6.0 0.7 %copy-done.6 = s32[1,4]{1,0:T(1,128)S(1)} copy-done((s32[1,4]{1,0:T(1,128)S(1)}, s32[1,4]{1,0:T(1,128)}, u32[]{:S(2)}) %copy-start.6) | copy-done | bytes 40
  6.7 0.0 copy-start.7
  6.7 0.7 %copy-done.7 = s32[1,4]{1,0:T(1,128)S(1)} copy-done((s32[1,4]{1,0:T(1,128)S(1)}, s32[1,4]{1,0:T(1,128)}, u32[]{:S(2)}) %copy-start.7) | copy-done | bytes 40
  7.3 0.0 copy-start.8
  7.3 0.7 %copy-done.8 = s32[128]{0:T(128)S(1)} copy-done((s32[128]{0:T(128)S(1)}, s32[128]{0:T(128)}, u32[]{:S(2)}) %copy-start.8) | copy-done | bytes 536
  8.0 45.0 %shard_map.91 = bf16[256,512]{1,0:T(8,128)(2,1)S(1)} custom-call(s32[1,4]{1,0:T(1,128)S(1)} %copy-done.6, s32[1,4]{1,0:T(1,128)S(1)} %copy-done.7, s32[128]{0:T(128)S(1)} %copy-done.8, bf16[256,512]{1,0:T(8,128)(2,1)S(1)} %copy-done.1, bf16[256,512]{1,0:T(8,128)(2,1)S(1)} %copy-done.2, bf16[256,512]{1,0:T(8,128)(2,1)S(1)} %copy-done.3, ...), custom_call_target="tpu_custom_call" | custom-call | tf_op jit(solution)/shard_map/pallas_call | solution.py:343
  53.0 0.7 %copy.11 = bf16[256,512]{1,0:T(8,128)(2,1)} copy(bf16[256,512]{1,0:T(8,128)(2,1)S(1)} %shard_map.91) | data formatting | bytes 524288
Async XLA Ops:
  0.0 1.6 %copy-start = (bf16[512,2048]{1,0:T(8,128)(2,1)S(1)}, bf16[512,2048]{1,0:T(8,128)(2,1)}, u32[]{:S(2)}) copy-start(bf16[512,2048]{1,0:T(8,128)(2,1)} %w_h.1) | copy-start | bytes 6291460
  1.6 0.9 %copy-start.1 = (bf16[256,512]{1,0:T(8,128)(2,1)S(1)}, bf16[256,512]{1,0:T(8,128)(2,1)}, u32[]{:S(2)}) copy-start(bf16[256,512]{1,0:T(8,128)(2,1)} %q_h.1) | copy-start | bytes 786436
  2.5 0.9 %copy-start.2 = (bf16[256,512]{1,0:T(8,128)(2,1)S(1)}, bf16[256,512]{1,0:T(8,128)(2,1)}, u32[]{:S(2)}) copy-start(bf16[256,512]{1,0:T(8,128)(2,1)} %k_h.1) | copy-start | bytes 786436
  3.5 0.9 %copy-start.3 = (bf16[256,512]{1,0:T(8,128)(2,1)S(1)}, bf16[256,512]{1,0:T(8,128)(2,1)}, u32[]{:S(2)}) copy-start(bf16[256,512]{1,0:T(8,128)(2,1)} %v_h.1) | copy-start | bytes 786436
  4.4 0.8 %copy-start.4 = (bf16[1,16,2048]{2,1,0:T(8,128)(2,1)S(1)}, bf16[1,16,2048]{2,1,0:T(8,128)(2,1)}, u32[]{:S(2)}) copy-start(bf16[1,16,2048]{2,1,0:T(8,128)(2,1)} %up_h.1) | copy-start | bytes 196612
  5.3 0.7 %copy-start.5 = (bf16[1,512,16]{1,2,0:T(8,128)(2,1)S(1)}, bf16[1,512,16]{1,2,0:T(8,128)(2,1)}, u32[]{:S(2)}) copy-start(bf16[1,512,16]{1,2,0:T(8,128)(2,1)} %param.15) | copy-start | bytes 49156
  6.0 0.7 %copy-start.6 = (s32[1,4]{1,0:T(1,128)S(1)}, s32[1,4]{1,0:T(1,128)}, u32[]{:S(2)}) copy-start(s32[1,4]{1,0:T(1,128)} %len_s.1) | copy-start | bytes 52
  6.7 0.7 %copy-start.7 = (s32[1,4]{1,0:T(1,128)S(1)}, s32[1,4]{1,0:T(1,128)}, u32[]{:S(2)}) copy-start(s32[1,4]{1,0:T(1,128)} %ids_s.1) | copy-start | bytes 52
  7.3 0.7 %copy-start.8 = (s32[128]{0:T(128)S(1)}, s32[128]{0:T(128)}, u32[]{:S(2)}) copy-start(s32[128]{0:T(128)} %home_s.1) | copy-start | bytes 1540

commit v2 on v1

--- a/solution.py
+++ b/solution.py
@@ -377,7 +377,7 @@
             dma((3,)),
         ],
         compiler_params=pltpu.CompilerParams(
-            collective_id=0, has_side_effects=True, vmem_limit_bytes=48 * 1024 * 1024
+            collective_id=0, has_side_effects=True, vmem_limit_bytes=67_043_328
         ),
     )(
         lengths,

time: 54 us -> 47.7 us (0.88)
  local copies, waits for them, and re-layouts: 8.66 us -> 1.67 us
  Pallas kernels: 45 us -> 45.8 us
    unnamed x19 -> x1, local copies, waits for them, and re-layouts: 8.66 us -> 1.67 us
    pallas_call x1, Pallas kernels: 45 us -> 45.8 us  [body(): pl.pallas_call(kernel, out_shape=jax.ShapeDtypeStruct((rows, width), BF16...]
where the time goes in v2:
time: 47.7 us; the launch traced here: 47.5 us
  Pallas kernels  45.8 us (96%)
  local copies, waits for them, and re-layouts  1.67 us (4%)
    pallas_call x1, Pallas kernels, body(): pl.pallas_call(kernel, out_shape=jax.ShapeDtypeStruct((rows, width), BF16...  45.8 us
    unnamed x1, local copies, waits for them, and re-layouts  1.67 us

profile of v2, /device:TPU:1, one launch (start us, length us, event | category | flops | bytes accessed | tf_op | source)
XLA Modules:
  0.0 47.5 jit_solution(23200949771024536)
XLA Ops:
  0.0 45.8 %shard_map.91 = bf16[256,512]{1,0:T(8,128)(2,1)} custom-call(s32[1,4]{1,0:T(1,128)} %len_s.1, s32[1,4]{1,0:T(1,128)} %ids_s.1, s32[128]{0:T(128)} %home_s.1, bf16[256,512]{1,0:T(8,128)(2,1)} %q_h.1, bf16[256,512]{1,0:T(8,128)(2,1)} %k_h.1, bf16[256,512]{1,0:T(8,128)(2,1)} %v_h.1, bf16[1,16,512]{2,1,0:T(8,128)(2,1)} %bitcast.1, bf16[1,16,2048]{2,1,0:T(8,128)(2,1)} %up_h.1, ...), custom_call_target="tpu_custom_call" | custom-call | tf_op jit(solution)/shard_map/pallas_call | solution.py:343
  45.8 1.7 %copy.11 = bf16[256,512]{1,0:T(8,128)(2,1)} copy(bf16[256,512]{1,0:T(8,128)(2,1)} %shard_map.91) | data formatting | bytes 524288

commit v3 on v0

v3 whole, which is shorter than its diff:
```python
import math

import jax
import jax.numpy as jnp
from jax import lax
from jax.experimental import pallas as pl
from jax.experimental.pallas import tpu as pltpu
from jax.sharding import PartitionSpec as P

HD = 128
NY, NZ, NX = 4, 16, 4
LINE = NY * NZ
MESH = pl.DeviceIdType.MESH
F32 = jnp.float32
BF16 = jnp.bfloat16

DOWN_TREE = {0: (4, 2, 1), 2: (3,), 4: (8, 6, 5), 6: (7,)}
UP_TREE = {0: (2, 1), 2: (4, 3), 4: (6, 5), 6: (8, 7)}


def offsets_at(distance):
    return (distance,) if distance in (0, NZ // 2) else (NZ - distance, distance)


def kernel(
    len_h,
    ids_h,
    home_h,
    q_h,
    k_h,
    v_h,
    dn_h,
    up_h,
    w_h,
    out_ref,
    len_s,
    ids_s,
    home_s,
    qv,
    kv,
    vv,
    wv,
    gd,
    gu,
    att,
    att_other,
    part,
    got,
    fwd_part,
    acc,
    note_all,
    note_s,
    pre_send,
    pre_got,
    up_send,
    up_got,
    low_send_buf,
    low_got,
    load_sem,
    d_send,
    u_send,
    zd_recv,
    zu_recv,
    y_recv,
    o_recv,
    x_send,
    x_recv,
    note_send,
    note_recv,
    att_sem,
    pre_sem,
    up_sem_send,
    up_sem_recv,
    low_send,
    low_recv,
):
    req = lax.axis_index("req")
    x = lax.axis_index("tp")
    core = lax.rem(req, 2)
    z = lax.rem(lax.div(req, 2), NZ)
    y = lax.div(req, 2 * NZ)
    rows, width = qv.shape
    half = rows // 2
    prompts = ids_s.shape[1]
    rank = gd.shape[1]

    def place(y_at, z_at, core_at):
        return (y_at * NZ + z_at) * 2 + core_at

    def shifted(at, by, size):
        return lax.rem(at + by % size, size)

    def z_peer(by):
        return (place(y, shifted(z, by, NZ), core), x)

    def y_peer(by, other=0):
        return (place(shifted(y, by, NY), z, 1 - core if other else core), x)

    def x_peer(by, other=0):
        return (place(y, z, 1 - core if other else core), shifted(x, by, NX))

    partner = y_peer(0, 1)

    def line(y_by, offset):
        return shifted(y, y_by, NY) * NZ + shifted(z, offset, NZ)

    def remote(src, dst, send, recv, device):
        return pltpu.make_async_remote_copy(
            src_ref=src, dst_ref=dst, send_sem=send, recv_sem=recv, device_id=device, device_id_type=MESH
        )

    plane = [(by, other) for by in range(NY) for other in range(2) if (by, other) != (0, 0)]

    columns = pl.ds(pl.multiple_of(x * width, width), width)
    loads = [
        pltpu.make_async_copy(dn_h.at[0], gd.at[line(0, 0)], load_sem.at[0]),
        pltpu.make_async_copy(up_h.at[0, :, columns], gu.at[z], load_sem.at[1]),
        pltpu.make_async_copy(len_h, len_s, load_sem.at[2]),
        pltpu.make_async_copy(ids_h, ids_s, load_sem.at[3]),
        pltpu.make_async_copy(home_h, home_s, load_sem.at[4]),
        pltpu.make_async_copy(q_h, qv, load_sem.at[5]),
        pltpu.make_async_copy(k_h, kv, load_sem.at[6]),
        pltpu.make_async_copy(v_h, vv, load_sem.at[7]),
        pltpu.make_async_copy(w_h, wv, load_sem.at[8]),
    ]
    for load in loads:
        load.start()
    barrier = pltpu.get_barrier_semaphore()
    peers = [z_peer(b) for b in (4, -4, 2, -2, 1, -1)] + [y_peer(b, o) for b, o in plane]
    peers += [x_peer(b, o) for b in range(1, NX) for o in range(2)]
    for peer in peers:
        pl.semaphore_signal(barrier, inc=1, device_id=peer, device_id_type=MESH)
    loads[0].wait()
    pl.semaphore_wait(barrier, len(peers))

    def z_bank(p, offset):
        return gu.at[shifted(z, offset, NZ)] if p else gd.at[line(0, offset)]

    z_recv = (zd_recv, zu_recv)
    z_send_sem = (d_send, u_send)
    trees = (DOWN_TREE, UP_TREE)

    def z_pass(p, offset):
        distance = min(offset, NZ - offset)
        for target in trees[p].get(distance, ()):
            for sign in (1, -1):
                if target == NZ // 2 and sign < 0:
                    continue
                if distance and (offset > NZ // 2) != (sign > 0):
                    continue
                by = sign * (target - distance)
                bank = z_bank(p, offset)
                remote(bank, bank, z_send_sem[p], z_recv[p].at[(offset - by) % NZ], z_peer(by)).start()

    def y_pass(offset):
        bank = gd.at[line(0, offset)]
        for way, by in ((0, 1), (1, -1)):
            remote(bank, bank, d_send, y_recv.at[way, offset], y_peer(by)).start()

    def z_take(p, *distances):
        for distance in distances:
            for offset in offsets_at(distance):
                bank = z_bank(p, offset)
                remote(bank, bank, z_send_sem[p], z_recv[p].at[offset], z_peer(1)).wait_recv()
                z_pass(p, offset)
                if p == 0:
                    y_pass(offset)

    def y_take(*distances):
        for distance in distances:
            for offset in offsets_at(distance):
                for way, by in ((0, 1), (1, -1)):
                    bank = gd.at[line(-by, offset)]
                    remote(bank, bank, d_send, y_recv.at[way, offset], y_peer(by)).wait_recv()
                    if (distance % 2 if distance < NZ // 2 else offset // NZ) == way:
                        remote(bank, bank, d_send, o_recv.at[offset], y_peer(by)).start()

    def o_take(*distances):
        for distance in distances:
            for offset in offsets_at(distance):
                bank = gd.at[line(2, offset)]
                remote(bank, bank, d_send, o_recv.at[offset], y_peer(1)).wait_recv()

    z_pass(0, 0)
    y_pass(0)
    loads[1].wait()
    z_pass(1, 0)

    for load in loads[2:5]:
        load.wait()
    starts = []
    edge = jnp.int32(0)
    for s in range(prompts - 1):
        edge = edge + len_s[0, s]
        starts.append(edge)
    homes = [home_s[ids_s[0, s]] for s in range(prompts)]
    lane = lax.broadcasted_iota(jnp.int32, (8, 128), 1)
    note = jnp.zeros((8, 128), jnp.int32)
    for i, value in enumerate(homes + starts):
        note = jnp.where(lane == i, value, note)
    note_all[0] = note
    notes = []
    for i, (by, other) in enumerate(plane):
        spot = 2 * ((NY - by) % NY) + other
        notes.append(remote(note_all.at[0], note_all.at[spot], note_send.at[i], note_recv.at[i], y_peer(by, other)))
    for copy in notes:
        copy.start()

    def allowed_of(first, count, keys):
        row = lax.broadcasted_iota(jnp.int32, (count, keys), 0) + first
        key = lax.broadcasted_iota(jnp.int32, (count, keys), 1)
        begin = jnp.zeros((count, keys), jnp.int32)
        for start in starts:
            begin = jnp.where(row >= start, start, begin)
        return (key <= row) & (key >= begin)

    def attend(first, keys):
        allowed = allowed_of(first, half, keys)
        for head in range(width // HD):
            cols = slice(head * HD, (head + 1) * HD)
            scores = lax.dot_general(
                qv[first : first + half, cols],
                kv[:keys, cols],
                (((1,), (1,)), ((), ())),
                preferred_element_type=F32,
            ) * (1.0 / math.sqrt(HD))
            masked = jnp.where(allowed, scores, -1e30)
            highest = jnp.max(masked, axis=1, keepdims=True)
            exponent = jnp.exp(masked - highest)
            weights = (exponent * (1.0 / jnp.sum(exponent, axis=1, keepdims=True))).astype(BF16)
            mixed = jnp.dot(weights, vv[:keys, cols], preferred_element_type=F32)
            att[first : first + half, cols] = mixed.astype(BF16)

    def project(first, count, by):
        cols = pl.ds(pl.multiple_of(shifted(x, by, NX) * width, width), width)
        return jnp.dot(att[first : first + count, :], wv[:, cols], preferred_element_type=F32)

    top, low = slice(0, half), slice(half, rows)

    def x_copy(slot, src, dst, by):
        return remote(src, dst, x_send.at[slot], x_recv.at[slot], x_peer(by))

    xc = (
        x_copy(0, part.at[0, top], fwd_part.at[top], 1),
        x_copy(1, part.at[0, low], fwd_part.at[low], -1),
        x_copy(2, part.at[1, top], got.at[0, top], 1),
        x_copy(3, part.at[1, low], got.at[0, low], 1),
        x_copy(4, part.at[2, top], got.at[1, top], -1),
        x_copy(5, part.at[2, low], got.at[1, low], -1),
    )

    for load in loads[5:8]:
        load.wait()
    attend(0, half)
    loads[8].wait()
    part[0, top] = project(0, half, 2).astype(BF16)
    xc[0].start()
    z_take(0, 1, 2)
    attend(half, rows)
    part[0, low] = project(half, half, 2).astype(BF16)
    xc[1].start()
    att_copy = remote(att, att_other, att_sem.at[0], att_sem.at[1], partner)
    att_copy.start()
    part[1, low] = project(half, half, 1).astype(BF16)
    xc[3].start()
    part[2, top] = project(0, half, -1).astype(BF16)
    xc[4].start()
    z_take(0, 4)
    z_take(1, 2, 1)
    z_take(0, 3)
    y_take(0, 1, 2)
    part[1, top] = project(0, half, 1).astype(BF16)
    part[2, low] = project(half, half, -1).astype(BF16)
    acc[...] = project(0, rows, 0)
    for copy in notes:
        copy.wait()
    notes_local = pltpu.make_async_copy(note_all, note_s, load_sem.at[9])
    notes_local.start()
    xc[0].wait_recv()
    part[1, top] = (part[1, top].astype(F32) + fwd_part[top].astype(F32)).astype(BF16)
    xc[2].start()
    xc[1].wait_recv()
    part[2, low] = (part[2, low].astype(F32) + fwd_part[low].astype(F32)).astype(BF16)
    xc[5].start()
    z_take(1, 4, 3)
    z_take(0, 5, 6)
    y_take(3, 4)
    z_take(0, 8, 7)
    z_take(1, 6, 5)
    y_take(5, 6)
    notes_local.wait()
    z_take(1, 8, 7)

    def pick_up(spot, s):
        home = note_s[spot, 0, s]
        mine = (lax.rem(home, 2) == core) & (lax.div(home, 2 * NZ) == y)
        return jnp.where(mine, gu[lax.rem(lax.div(home, 2), NZ)], 0).astype(BF16)

    for by in range(NY):
        for s in range(prompts):
            pre_send[by, s] = pick_up(2 * by + 1, s)
    pre = remote(pre_send, pre_got, pre_sem.at[0], pre_sem.at[1], partner)
    pre.start()
    for by in range(NY):
        for s in range(prompts):
            up_send[by, s] = pick_up(2 * by, s)
    y_take(8, 7)
    pre.wait()
    ups = []
    for by in (2, 1, 3):
        up_send[by] = up_send[by] + pre_got[by]
        ups.append(remote(up_send.at[by], up_got.at[by - 1], up_sem_send.at[by - 1], up_sem_recv.at[by - 1], y_peer(by)))
        ups[-1].start()
    for c in (2, 3, 4, 5):
        xc[c].wait_recv()
    acc[...] += got[0].astype(F32) + got[1].astype(F32)
    att_copy.wait()
    o_take(0, 1, 2, 3, 4, 5, 6, 8, 7)

    token = lax.broadcasted_iota(jnp.int32, (rank, rows), 1)

    def in_prompt(s, begins):
        inside = token >= begins[s - 1] if s else token >= 0
        return inside & (token < begins[s]) if s < prompts - 1 else inside

    def low_rank(spot, rows_ref):
        factors = []
        for s in range(prompts):
            home = note_s[spot, 0, s]
            factors.append(jnp.where(lax.rem(home, 2) == core, gd[lax.div(home, 2)], 0).astype(BF16))
        begins = [note_s[spot, 0, prompts + s] for s in range(prompts - 1)]
        every = lax.dot_general(
            jnp.concatenate(factors, axis=0), rows_ref[...], (((1,), (1,)), ((), ())), preferred_element_type=F32
        )
        total = jnp.zeros((rank, rows), F32)
        for s in range(prompts):
            total = total + jnp.where(in_prompt(s, begins), every[s * rank : (s + 1) * rank, :], 0.0)
        return total

    low_send_buf[0] = low_rank(0, att)
    lows = []

    def low_copy(which, spot, device):
        copy = remote(low_send_buf.at[which], low_got.at[spot], low_send.at[spot], low_recv.at[spot], device)
        copy.start()
        lows.append(copy)

    for by in (2, 1, 3):
        low_copy(0, by - 1, x_peer(by))
    low_send_buf[1] = low_rank(1, att_other)
    for by in (2, 1, 3, 0):
        low_copy(1, by + 3, x_peer(by, 1))

    factor_up = up_send[0] + pre_got[0]
    for copy in ups:
        copy.wait()
    factor_up = (factor_up + up_got[0]) + (up_got[1] + up_got[2])
    factor_up = factor_up.reshape(prompts * rank, width)
    for copy in lows:
        copy.wait()
    total = low_send_buf[0]
    for spot in range(7):
        total = total + low_got[spot]
    spread = jnp.concatenate([jnp.where(in_prompt(s, starts), total, 0.0) for s in range(prompts)], axis=0).T
    high = spread.astype(BF16)
    rest = (spread - high.astype(F32)).astype(BF16)
    delta = jnp.dot(high, factor_up, preferred_element_type=F32) + jnp.dot(
        rest, factor_up, preferred_element_type=F32
    )
    out_ref[...] = (acc[...] + delta).astype(BF16)

    for copy in xc:
        copy.wait_send()
    sent = gd.at[pl.ds(0, LINE - 1)]
    remote(sent, sent, d_send, d_send, z_peer(1)).wait_send()
    sent = gu.at[pl.ds(0, NZ - 1)]
    remote(sent, sent, u_send, u_send, z_peer(1)).wait_send()


def body(queries, key_rows, value_rows, lengths, adapter_ids, adapter_home, adapter_down, adapter_up, output_weight):
    rows, width = queries.shape
    rank = adapter_up.shape[1]
    prompts = lengths.shape[1]
    dma = pltpu.SemaphoreType.DMA
    hbm = pl.BlockSpec(memory_space=pltpu.HBM)
    block = pltpu.VMEM((rows, width), BF16)
    return pl.pallas_call(
        kernel,
        out_shape=jax.ShapeDtypeStruct((rows, width), BF16),
        in_specs=[hbm] * 9,
        out_specs=pl.BlockSpec(memory_space=pltpu.VMEM),
        scratch_shapes=[
            pltpu.SMEM(lengths.shape, jnp.int32),
            pltpu.SMEM(adapter_ids.shape, jnp.int32),
            pltpu.SMEM(adapter_home.shape, jnp.int32),
            block,
            block,
            block,
            pltpu.VMEM(output_weight.shape, BF16),
            pltpu.VMEM((LINE, rank, width), BF16),
            pltpu.VMEM((NZ, rank, width), BF16),
            block,
            block,
            pltpu.VMEM((3, rows, width), BF16),
            pltpu.VMEM((2, rows, width), BF16),
            block,
            pltpu.VMEM((rows, width), F32),
            pltpu.VMEM((2 * NY, 8, 128), jnp.int32),
            pltpu.SMEM((2 * NY, 8, 128), jnp.int32),
            pltpu.VMEM((NY, prompts, rank, width), BF16),
            pltpu.VMEM((NY, prompts, rank, width), BF16),
            pltpu.VMEM((NY, prompts, rank, width), BF16),
            pltpu.VMEM((NY - 1, prompts, rank, width), BF16),
            pltpu.VMEM((2, rank, rows), F32),
            pltpu.VMEM((7, rank, rows), F32),
            dma((10,)),
            dma,
            dma,
            dma((NZ,)),
            dma((NZ,)),
            dma((2, NZ)),
            dma((NZ,)),
            dma((6,)),
            dma((6,)),
            dma((7,)),
            dma((7,)),
            dma((2,)),
            dma((2,)),
            dma((3,)),
            dma((3,)),
            dma((7,)),
            dma((7,)),
        ],
        compiler_params=pltpu.CompilerParams(
            collective_id=0, has_side_effects=True, vmem_limit_bytes=VMEM_LIMIT
        ),
    )(
        lengths,
        adapter_ids,
        adapter_home,
        queries,
        key_rows,
        value_rows,
        jnp.swapaxes(adapter_down, 1, 2),
        adapter_up,
        output_weight,
    )


VMEM_LIMIT = 67_043_328


def solution(mesh):
    return jax.shard_map(
        body,
        mesh=mesh,
        in_specs=(
            P("req", "tp"),
            P("req", "tp"),
            P("req", "tp"),
            P("req", None),
            P("req", None),
            P(),
            P("req", "tp", None),
            P("req", None, None),
            P("tp", None),
        ),
        out_specs=P("req", "tp"),
        check_vma=False,
    )
```

time: 351 us -> 46.5 us (0.13)
  waiting for transfers between devices: 317 us -> 0 us
  Pallas kernels: 0 us -> 44.7 us
  between operations: 13.2 us -> 0.01 us
  matrix products: 7.58 us -> 0 us
  local copies, waits for them, and re-layouts: 9.21 us -> 1.67 us
    all_gather x2 -> x0, waiting for transfers between devices: 284 us -> none  [the longest x1 144 us: body(): lax.all_gather(adapter_up, 'req', axis=0, tiled=True)]
    pallas_call x0 -> x1, Pallas kernels: none -> 44.7 us  [body(): pl.pallas_call(kernel, out_shape=jax.ShapeDtypeStruct((rows, width), BF16...]
    reduce_scatter x1 -> x0, waiting for transfers between devices: 31.8 us -> none  [body(): lax.psum_scatter(partial_rows, 'tp', scatter_dimension=1, tiled=True)]
    gather x3 -> x0, local copies, waits for them, and re-layouts: 7.37 us -> none  [the longest x1 3.94 us: body(): uppers = uppers_all[slot_rows]]
    dot_general x5 -> x0, matrix products: 5.98 us -> none  [the longest x1 2.1 us: body(): jnp.dot(attended, output_weight, preferred_element_type=jnp.float32)]
  transfers between devices with their start and end apart: 3 -> 0, of which waited for: 3 -> 0; matrix products, arithmetic and copies ran while one was open for 3% -> 0% of each run, Pallas kernels for 0% -> 0%
where the time goes in v3:
time: 46.5 us; the launch traced here: 46.4 us
  Pallas kernels  44.7 us (96%)
  local copies, waits for them, and re-layouts  1.67 us (4%)
    pallas_call x1, Pallas kernels, body(): pl.pallas_call(kernel, out_shape=jax.ShapeDtypeStruct((rows, width), BF16...  44.7 us
    unnamed x1, local copies, waits for them, and re-layouts  1.67 us

profile of v3, /device:TPU:1, one launch (start us, length us, event | category | flops | bytes accessed | tf_op | source)
XLA Modules:
  0.0 46.4 jit_solution(10184199451291694791)
XLA Ops:
  0.0 44.7 %shard_map.91 = bf16[256,512]{1,0:T(8,128)(2,1)} custom-call(s32[1,4]{1,0:T(1,128)} %len_h.1, s32[1,4]{1,0:T(1,128)} %ids_h.1, s32[128]{0:T(128)} %home_h.1, bf16[256,512]{1,0:T(8,128)(2,1)} %q_h.1, bf16[256,512]{1,0:T(8,128)(2,1)} %k_h.1, bf16[256,512]{1,0:T(8,128)(2,1)} %v_h.1, bf16[1,16,512]{2,1,0:T(8,128)(2,1)} %bitcast.1, bf16[1,16,2048]{2,1,0:T(8,128)(2,1)} %up_h.1, ...), custom_call_target="tpu_custom_call" | custom-call | tf_op jit(solution)/shard_map/pallas_call | solution.py:387
  44.7 1.7 %copy.11 = bf16[256,512]{1,0:T(8,128)(2,1)} copy(bf16[256,512]{1,0:T(8,128)(2,1)} %shard_map.91) | data formatting | bytes 524288

commit v4 on v3

--- a/solution.py
+++ b/solution.py
@@ -14,8 +14,7 @@
 F32 = jnp.float32
 BF16 = jnp.bfloat16
 
-DOWN_TREE = {0: (4, 2, 1), 2: (3,), 4: (8, 6, 5), 6: (7,)}
-UP_TREE = {0: (2, 1), 2: (4, 3), 4: (6, 5), 6: (8, 7)}
+TREE = {0: (4, 2, 1), 2: (3,), 4: (8, 6, 5), 6: (7,)}
 
 
 def offsets_at(distance):
@@ -50,8 +49,6 @@
     acc,
     note_all,
     note_s,
-    pre_send,
-    pre_got,
     up_send,
     up_got,
     low_send_buf,
@@ -68,7 +65,8 @@
     note_send,
     note_recv,
     att_sem,
-    pre_sem,
+    piece_send,
+    piece_recv,
     up_sem_send,
     up_sem_recv,
     low_send,
@@ -111,10 +109,17 @@
 
     plane = [(by, other) for by in range(NY) for other in range(2) if (by, other) != (0, 0)]
 
-    columns = pl.ds(pl.multiple_of(x * width, width), width)
+    seat = 2 * y + core
+    tile = width // NY
+
+    def piece_of(by, other):
+        first = pl.multiple_of((1 - core if other else core) * (rank // 2), rank // 2)
+        column = pl.multiple_of(x * width + shifted(y, by, NY) * tile, tile)
+        return up_h.at[0, pl.ds(first, rank // 2), pl.ds(column, tile)]
+
     loads = [
         pltpu.make_async_copy(dn_h.at[0], gd.at[line(0, 0)], load_sem.at[0]),
-        pltpu.make_async_copy(up_h.at[0, :, columns], gu.at[z], load_sem.at[1]),
+        pltpu.make_async_copy(piece_of(0, 0), gu.at[z, seat], load_sem.at[1]),
         pltpu.make_async_copy(len_h, len_s, load_sem.at[2]),
         pltpu.make_async_copy(ids_h, ids_s, load_sem.at[3]),
         pltpu.make_async_copy(home_h, home_s, load_sem.at[4]),
@@ -138,11 +143,10 @@
 
     z_recv = (zd_recv, zu_recv)
     z_send_sem = (d_send, u_send)
-    trees = (DOWN_TREE, UP_TREE)
 
     def z_pass(p, offset):
         distance = min(offset, NZ - offset)
-        for target in trees[p].get(distance, ()):
+        for target in TREE.get(distance, ()):
             for sign in (1, -1):
                 if target == NZ // 2 and sign < 0:
                     continue
@@ -183,8 +187,12 @@
 
     z_pass(0, 0)
     y_pass(0)
-    loads[1].wait()
-    z_pass(1, 0)
+    pieces = [
+        remote(piece_of(by, other), gu.at[z, seat], piece_send.at[i], piece_recv.at[i], y_peer(by, other))
+        for i, (by, other) in enumerate(plane)
+    ]
+    for copy in pieces:
+        copy.start()
 
     for load in loads[2:5]:
         load.wait()
@@ -256,6 +264,10 @@
     part[0, top] = project(0, half, 2).astype(BF16)
     xc[0].start()
     z_take(0, 1, 2)
+    loads[1].wait()
+    for copy in pieces:
+        copy.wait()
+    z_pass(1, 0)
     attend(half, rows)
     part[0, low] = project(half, half, 2).astype(BF16)
     xc[1].start()
@@ -265,9 +277,7 @@
     xc[3].start()
     part[2, top] = project(0, half, -1).astype(BF16)
     xc[4].start()
-    z_take(0, 4)
-    z_take(1, 2, 1)
-    z_take(0, 3)
+    z_take(0, 4, 3)
     y_take(0, 1, 2)
     part[1, top] = project(0, half, 1).astype(BF16)
     part[2, low] = project(half, half, -1).astype(BF16)
@@ -282,35 +292,27 @@
     xc[1].wait_recv()
     part[2, low] = (part[2, low].astype(F32) + fwd_part[low].astype(F32)).astype(BF16)
     xc[5].start()
-    z_take(1, 4, 3)
+    z_take(1, 1, 2, 4)
     z_take(0, 5, 6)
     y_take(3, 4)
     z_take(0, 8, 7)
-    z_take(1, 6, 5)
-    y_take(5, 6)
+    z_take(1, 3)
     notes_local.wait()
-    z_take(1, 8, 7)
+    y_take(5, 6, 8, 7)
+    z_take(1, 5, 6, 8, 7)
 
     def pick_up(spot, s):
         home = note_s[spot, 0, s]
-        mine = (lax.rem(home, 2) == core) & (lax.div(home, 2 * NZ) == y)
-        return jnp.where(mine, gu[lax.rem(lax.div(home, 2), NZ)], 0).astype(BF16)
-
-    for by in range(NY):
+        return gu[lax.rem(lax.div(home, 2), NZ), 2 * lax.div(home, 2 * NZ) + lax.rem(home, 2)]
+
+    ups = []
+    for i, (by, other) in enumerate(plane):
         for s in range(prompts):
-            pre_send[by, s] = pick_up(2 * by + 1, s)
-    pre = remote(pre_send, pre_got, pre_sem.at[0], pre_sem.at[1], partner)
-    pre.start()
-    for by in range(NY):
-        for s in range(prompts):
-            up_send[by, s] = pick_up(2 * by, s)
-    y_take(8, 7)
-    pre.wait()
-    ups = []
-    for by in (2, 1, 3):
-        up_send[by] = up_send[by] + pre_got[by]
-        ups.append(remote(up_send.at[by], up_got.at[by - 1], up_sem_send.at[by - 1], up_sem_recv.at[by - 1], y_peer(by)))
+            up_send[i, s] = pick_up(2 * by + other, s)
+        ups.append(remote(up_send.at[i], up_got.at[seat], up_sem_send.at[i], up_sem_recv.at[i], y_peer(by, other)))
         ups[-1].start()
+    for s in range(prompts):
+        up_got[seat, s] = pick_up(0, s)
     for c in (2, 3, 4, 5):
         xc[c].wait_recv()
     acc[...] += got[0].astype(F32) + got[1].astype(F32)
@@ -351,11 +353,16 @@
     for by in (2, 1, 3, 0):
         low_copy(1, by + 3, x_peer(by, 1))
 
-    factor_up = up_send[0] + pre_got[0]
     for copy in ups:
         copy.wait()
-    factor_up = (factor_up + up_got[0]) + (up_got[1] + up_got[2])
-    factor_up = factor_up.reshape(prompts * rank, width)
+    factor_up = jnp.concatenate(
+        [
+            jnp.concatenate([up_got[2 * quarter + part_of, s].astype(F32) for quarter in range(NY)], axis=1)
+            for s in range(prompts)
+            for part_of in range(2)
+        ],
+        axis=0,
+    ).astype(BF16)
     for copy in lows:
         copy.wait()
     total = low_send_buf[0]
@@ -398,7 +405,7 @@
             block,
             pltpu.VMEM(output_weight.shape, BF16),
             pltpu.VMEM((LINE, rank, width), BF16),
-            pltpu.VMEM((NZ, rank, width), BF16),
+            pltpu.VMEM((NZ, 2 * NY, rank // 2, width // NY), BF16),
             block,
             block,
             pltpu.VMEM((3, rows, width), BF16),
@@ -407,10 +414,8 @@
             pltpu.VMEM((rows, width), F32),
             pltpu.VMEM((2 * NY, 8, 128), jnp.int32),
             pltpu.SMEM((2 * NY, 8, 128), jnp.int32),
-            pltpu.VMEM((NY, prompts, rank, width), BF16),
-            pltpu.VMEM((NY, prompts, rank, width), BF16),
-            pltpu.VMEM((NY, prompts, rank, width), BF16),
-            pltpu.VMEM((NY - 1, prompts, rank, width), BF16),
+            pltpu.VMEM((2 * NY - 1, prompts, rank // 2, width // NY), BF16),
+            pltpu.VMEM((2 * NY, prompts, rank // 2, width // NY), BF16),
             pltpu.VMEM((2, rank, rows), F32),
             pltpu.VMEM((7, rank, rows), F32),
             dma((10,)),
@@ -425,9 +430,10 @@
             dma((7,)),
             dma((7,)),
             dma((2,)),
-            dma((2,)),
-            dma((3,)),
-            dma((3,)),
+            dma((7,)),
+            dma((7,)),
+            dma((7,)),
+            dma((7,)),
             dma((7,)),
             dma((7,)),
         ],
@@ -435,19 +441,24 @@
             collective_id=0, has_side_effects=True, vmem_limit_bytes=VMEM_LIMIT
         ),
     )(
-        lengths,
-        adapter_ids,
-        adapter_home,
-        queries,
-        key_rows,
-        value_rows,
-        jnp.swapaxes(adapter_down, 1, 2),
-        adapter_up,
-        output_weight,
+        *(
+            pltpu.with_memory_space_constraint(operand, pltpu.HBM)
+            for operand in (
+                lengths,
+                adapter_ids,
+                adapter_home,
+                queries,
+                key_rows,
+                value_rows,
+                jnp.swapaxes(adapter_down, 1, 2),
+                adapter_up,
+                output_weight,
+            )
+        )
     )
 
 
-VMEM_LIMIT = 67_043_328
+VMEM_LIMIT = 40 * 1024 * 1024
 
 
 def solution(mesh):

time: 46.5 us -> 44.9 us (0.966)
  local copies, waits for them, and re-layouts: 1.67 us -> 0.71 us
  Pallas kernels: 44.7 us -> 44 us
    unnamed x1, local copies, waits for them, and re-layouts: 1.67 us -> 0.71 us
    pallas_call x1, Pallas kernels: 44.7 us -> 44 us  [body(): pl.pallas_call(kernel, out_shape=jax.ShapeDtypeStruct((rows, width), BF16...]
where the time goes in v4:
time: 44.9 us; the launch traced here: 44.7 us
  Pallas kernels  44 us (98%)
  local copies, waits for them, and re-layouts  0.71 us (2%)
    pallas_call x1, Pallas kernels, body(): pl.pallas_call(kernel, out_shape=jax.ShapeDtypeStruct((rows, width), BF16...  44 us

profile of v4, /device:TPU:1, one launch (start us, length us, event | category | flops | bytes accessed | tf_op | source)
XLA Modules:
  0.0 44.7 jit_solution(3081527439458410694)
XLA Ops:
  0.0 44.0 %shard_map.91 = bf16[256,512]{1,0:T(8,128)(2,1)S(1)} custom-call(s32[1,4]{1,0:T(1,128)} %len_h.1, s32[1,4]{1,0:T(1,128)} %ids_h.1, s32[128]{0:T(128)} %home_h.1, bf16[256,512]{1,0:T(8,128)(2,1)} %q_h.1, bf16[256,512]{1,0:T(8,128)(2,1)} %k_h.1, bf16[256,512]{1,0:T(8,128)(2,1)} %v_h.1, bf16[1,16,512]{2,1,0:T(8,128)(2,1)} %bitcast.1, ...), custom_call_target="tpu_custom_call" | custom-call | tf_op jit(solution)/shard_map/pallas_call | solution.py:394
  44.0 0.7 %copy.11 = bf16[256,512]{1,0:T(8,128)(2,1)} copy(bf16[256,512]{1,0:T(8,128)(2,1)S(1)} %shard_map.91) | data formatting | bytes 524288

commit v5 on v4

--- a/solution.py
+++ b/solution.py
@@ -14,7 +14,8 @@
 F32 = jnp.float32
 BF16 = jnp.bfloat16
 
-TREE = {0: (4, 2, 1), 2: (3,), 4: (8, 6, 5), 6: (7,)}
+DOWN_TREE = {0: (4, 2, 1), 2: (3,), 4: (8, 7, 6, 5)}
+UP_TREE = {0: (4, 2, 1), 2: (3,), 4: (8, 7, 6, 5)}
 
 
 def offsets_at(distance):
@@ -131,7 +132,7 @@
     for load in loads:
         load.start()
     barrier = pltpu.get_barrier_semaphore()
-    peers = [z_peer(b) for b in (4, -4, 2, -2, 1, -1)] + [y_peer(b, o) for b, o in plane]
+    peers = [z_peer(b) for b in (4, -4, 3, -3, 2, -2, 1, -1)] + [y_peer(b, o) for b, o in plane]
     peers += [x_peer(b, o) for b in range(1, NX) for o in range(2)]
     for peer in peers:
         pl.semaphore_signal(barrier, inc=1, device_id=peer, device_id_type=MESH)
@@ -146,7 +147,7 @@
 
     def z_pass(p, offset):
         distance = min(offset, NZ - offset)
-        for target in TREE.get(distance, ()):
+        for target in (UP_TREE if p else DOWN_TREE).get(distance, ()):
             for sign in (1, -1):
                 if target == NZ // 2 and sign < 0:
                     continue
@@ -158,6 +159,7 @@
 
     def y_pass(offset):
         bank = gd.at[line(0, offset)]
+        remote(bank, bank, d_send, o_recv.at[offset], y_peer(2)).start()
         for way, by in ((0, 1), (1, -1)):
             remote(bank, bank, d_send, y_recv.at[way, offset], y_peer(by)).start()
 
@@ -176,8 +178,6 @@
                 for way, by in ((0, 1), (1, -1)):
                     bank = gd.at[line(-by, offset)]
                     remote(bank, bank, d_send, y_recv.at[way, offset], y_peer(by)).wait_recv()
-                    if (distance % 2 if distance < NZ // 2 else offset // NZ) == way:
-                        remote(bank, bank, d_send, o_recv.at[offset], y_peer(by)).start()
 
     def o_take(*distances):
         for distance in distances:
@@ -263,11 +263,11 @@
     loads[8].wait()
     part[0, top] = project(0, half, 2).astype(BF16)
     xc[0].start()
-    z_take(0, 1, 2)
     loads[1].wait()
     for copy in pieces:
         copy.wait()
     z_pass(1, 0)
+    z_take(0, 1, 2)
     attend(half, rows)
     part[0, low] = project(half, half, 2).astype(BF16)
     xc[1].start()

time: 44.9 us -> 42.2 us (0.940)
  Pallas kernels: 44 us -> 41.3 us
    pallas_call x1, Pallas kernels: 44 us -> 41.3 us  [body(): pl.pallas_call(kernel, out_shape=jax.ShapeDtypeStruct((rows, width), BF16...]
where the time goes in v5:
time: 42.2 us; the launch traced here: 42 us
  Pallas kernels  41.3 us (98%)
  local copies, waits for them, and re-layouts  0.71 us (2%)
    pallas_call x1, Pallas kernels, body(): pl.pallas_call(kernel, out_shape=jax.ShapeDtypeStruct((rows, width), BF16...  41.3 us

profile of v5, /device:TPU:1, one launch (start us, length us, event | category | flops | bytes accessed | tf_op | source)
XLA Modules:
  0.0 42.0 jit_solution(14043265658076687489)
XLA Ops:
  0.0 41.3 %shard_map.91 = bf16[256,512]{1,0:T(8,128)(2,1)S(1)} custom-call(s32[1,4]{1,0:T(1,128)} %len_h.1, s32[1,4]{1,0:T(1,128)} %ids_h.1, s32[128]{0:T(128)} %home_h.1, bf16[256,512]{1,0:T(8,128)(2,1)} %q_h.1, bf16[256,512]{1,0:T(8,128)(2,1)} %k_h.1, bf16[256,512]{1,0:T(8,128)(2,1)} %v_h.1, bf16[1,16,512]{2,1,0:T(8,128)(2,1)} %bitcast.1, ...), custom_call_target="tpu_custom_call" | custom-call | tf_op jit(solution)/shard_map/pallas_call | solution.py:394
  41.3 0.7 %copy.11 = bf16[256,512]{1,0:T(8,128)(2,1)} copy(bf16[256,512]{1,0:T(8,128)(2,1)S(1)} %shard_map.91) | data formatting | bytes 524288

commit v6 on v5

--- a/solution.py
+++ b/solution.py
@@ -149,7 +149,7 @@
         distance = min(offset, NZ - offset)
         for target in (UP_TREE if p else DOWN_TREE).get(distance, ()):
             for sign in (1, -1):
-                if target == NZ // 2 and sign < 0:
+                if target == NZ // 2 and sign != (-1 if p else 1):
                     continue
                 if distance and (offset > NZ // 2) != (sign > 0):
                     continue
@@ -186,13 +186,13 @@
                 remote(bank, bank, d_send, o_recv.at[offset], y_peer(1)).wait_recv()
 
     z_pass(0, 0)
-    y_pass(0)
     pieces = [
         remote(piece_of(by, other), gu.at[z, seat], piece_send.at[i], piece_recv.at[i], y_peer(by, other))
         for i, (by, other) in enumerate(plane)
     ]
     for copy in pieces:
         copy.start()
+    y_pass(0)
 
     for load in loads[2:5]:
         load.wait()
@@ -313,9 +313,6 @@
         ups[-1].start()
     for s in range(prompts):
         up_got[seat, s] = pick_up(0, s)
-    for c in (2, 3, 4, 5):
-        xc[c].wait_recv()
-    acc[...] += got[0].astype(F32) + got[1].astype(F32)
     att_copy.wait()
     o_take(0, 1, 2, 3, 4, 5, 6, 8, 7)
 
@@ -353,6 +350,9 @@
     for by in (2, 1, 3, 0):
         low_copy(1, by + 3, x_peer(by, 1))
 
+    for c in (2, 3, 4, 5):
+        xc[c].wait_recv()
+    acc[...] += got[0].astype(F32) + got[1].astype(F32)
     for copy in ups:
         copy.wait()
     factor_up = jnp.concatenate(

time: 42.2 us -> 41.7 us (0.988)
  Pallas kernels: 41.3 us -> 40.8 us
    pallas_call x1, Pallas kernels: 41.3 us -> 40.8 us  [body(): pl.pallas_call(kernel, out_shape=jax.ShapeDtypeStruct((rows, width), BF16...]
where the time goes in v6:
time: 41.7 us; the launch traced here: 41.5 us
  Pallas kernels  40.8 us (98%)
  local copies, waits for them, and re-layouts  0.71 us (2%)
    pallas_call x1, Pallas kernels, body(): pl.pallas_call(kernel, out_shape=jax.ShapeDtypeStruct((rows, width), BF16...  40.8 us

profile of v6, /device:TPU:1, one launch (start us, length us, event | category | flops | bytes accessed | tf_op | source)
XLA Modules:
  0.0 41.5 jit_solution(612540106563528248)
XLA Ops:
  0.0 40.8 %shard_map.91 = bf16[256,512]{1,0:T(8,128)(2,1)S(1)} custom-call(s32[1,4]{1,0:T(1,128)} %len_h.1, s32[1,4]{1,0:T(1,128)} %ids_h.1, s32[128]{0:T(128)} %home_h.1, bf16[256,512]{1,0:T(8,128)(2,1)} %q_h.1, bf16[256,512]{1,0:T(8,128)(2,1)} %k_h.1, bf16[256,512]{1,0:T(8,128)(2,1)} %v_h.1, bf16[1,16,512]{2,1,0:T(8,128)(2,1)} %bitcast.1, ...), custom_call_target="tpu_custom_call" | custom-call | tf_op jit(solution)/shard_map/pallas_call | solution.py:394
  40.8 0.7 %copy.11 = bf16[256,512]{1,0:T(8,128)(2,1)} copy(bf16[256,512]{1,0:T(8,128)(2,1)S(1)} %shard_map.91) | data formatting | bytes 524288

commit v7 on v6

--- a/solution.py
+++ b/solution.py
@@ -298,7 +298,6 @@
     z_take(0, 8, 7)
     z_take(1, 3)
     notes_local.wait()
-    y_take(5, 6, 8, 7)
     z_take(1, 5, 6, 8, 7)
 
     def pick_up(spot, s):
@@ -314,6 +313,7 @@
     for s in range(prompts):
         up_got[seat, s] = pick_up(0, s)
     att_copy.wait()
+    y_take(5, 6, 8, 7)
     o_take(0, 1, 2, 3, 4, 5, 6, 8, 7)
 
     token = lax.broadcasted_iota(jnp.int32, (rank, rows), 1)

time: 41.7 us -> 41.5 us (level)
  no operation moved by 1% of the time
where the time goes in v7:
time: 41.5 us; the launch traced here: 41.4 us
  Pallas kernels  40.7 us (98%)
  local copies, waits for them, and re-layouts  0.71 us (2%)
    pallas_call x1, Pallas kernels, body(): pl.pallas_call(kernel, out_shape=jax.ShapeDtypeStruct((rows, width), BF16...  40.7 us

profile of v7, /device:TPU:1, one launch (start us, length us, event | category | flops | bytes accessed | tf_op | source)
XLA Modules:
  0.0 41.4 jit_solution(10759410955873644502)
XLA Ops:
  0.0 40.7 %shard_map.91 = bf16[256,512]{1,0:T(8,128)(2,1)S(1)} custom-call(s32[1,4]{1,0:T(1,128)} %len_h.1, s32[1,4]{1,0:T(1,128)} %ids_h.1, s32[128]{0:T(128)} %home_h.1, bf16[256,512]{1,0:T(8,128)(2,1)} %q_h.1, bf16[256,512]{1,0:T(8,128)(2,1)} %k_h.1, bf16[256,512]{1,0:T(8,128)(2,1)} %v_h.1, bf16[1,16,512]{2,1,0:T(8,128)(2,1)} %bitcast.1, ...), custom_call_target="tpu_custom_call" | custom-call | tf_op jit(solution)/shard_map/pallas_call | solution.py:394
  40.7 0.7 %copy.11 = bf16[256,512]{1,0:T(8,128)(2,1)} copy(bf16[256,512]{1,0:T(8,128)(2,1)S(1)} %shard_map.91) | data formatting | bytes 524288
